TPU v7x, 512 devices: a whole 4x8x8 slice. The times are simulated.
512 devices in a mesh: sub: 16 (over z, core), tile: 32 (over y, x).
Axes of the slice: x: 4, y: 8, z: 8, core: 2. Of those that a mesh axis runs over, the one named last changes fastest.
Arguments:
- echoes: float32 [32, 32, 128], P('sub', 'tile'), may hold values from -6 to 6
- pulse_offset: float32 [32, 32], P('sub', 'tile'), may hold values from 0 to 1
- range_gates: int32 [32, 32, 64], P('sub', 'tile'), may hold values from 0 to 511
- visible: int32 [32, 256], P('sub', 'tile'), may hold values 0 or 1
Outputs:
- images: float32 [32, 256, 128, 256], P('sub', 'tile')
- peak: float32 [256, 128, 128], P('tile', 'sub')
All inputs are finite; a program needn't handle non-finite values. No bound on the sum of `visible` on one device may be relied on, other than what follows from the above.
Results may differ from a plain program's by a relative error of at most 0.0037.
Values sent between devices are 32-bit elements; how exact they have to be, the bound alone decides.
No kernel may reach another device: no remote copies, remote signals or barrier semaphores. Data moves between devices by JAX's collectives and lax.ppermute only.
A program may use at most 64 MiB of HBM per device.

v0:
```python
import math
import jax
import jax.numpy as jnp
from jax import lax
from jax.sharding import PartitionSpec as P

PULSE_H = 32
FREQS = 64
PIX = 128
GATES = 512
grid_cols = 16
two_pi = 2.0 * math.pi


def shifted(block, axis, distance):
    devices = range(lax.axis_size(axis))
    route = [((i - distance) % len(devices), i) for i in devices]
    return lax.ppermute(block, axis, route)


def make_right(sine_wave):
    pixels = jnp.arange(PIX, dtype=jnp.float32)
    phase_grid = sine_wave[:, None] * pixels[None, :]
    real_part = jnp.cos(phase_grid).astype(jnp.bfloat16)
    imag_part = jnp.sin(phase_grid).astype(jnp.bfloat16)
    upper = jnp.concatenate([real_part, imag_part], axis=1)
    lower = jnp.concatenate([-imag_part, real_part], axis=1)
    return jnp.concatenate([upper, lower], axis=0)


def make_base(cosine_wave):
    pixels = jnp.arange(PIX, dtype=jnp.float32)
    base_phase = cosine_wave[None, :] * pixels[:, None]
    return (jnp.cos(base_phase), jnp.sin(base_phase))


def make_left(
    echo_real, echo_imag, cosine_wave, sine_wave, base_cos, base_sin, tile_number, norm_scale
):
    column = (tile_number % grid_cols * PIX - 8 * PIX).astype(jnp.float32)
    row_start = (tile_number // grid_cols * PIX - 4 * PIX).astype(jnp.float32)
    offset_phase = cosine_wave * column + sine_wave * row_start
    offset_cos = jnp.cos(offset_phase)
    offset_sin = jnp.sin(offset_phase)
    turned_real = norm_scale * (echo_real * offset_cos - echo_imag * offset_sin)
    turned_imag = norm_scale * (echo_real * offset_sin + echo_imag * offset_cos)
    real_part = turned_real[None, :] * base_cos - turned_imag[None, :] * base_sin
    imag_part = turned_real[None, :] * base_sin + turned_imag[None, :] * base_cos
    return jnp.concatenate([real_part, imag_part], axis=1).astype(jnp.bfloat16)


def on_device(echoes, pulse_offset, range_gates, visible):
    half_dev = echoes.shape[0]
    tile_dev = visible.shape[1]
    sub_count = lax.axis_size("sub")
    half_total = half_dev * sub_count
    first_half = lax.axis_index("sub") * half_dev
    first_tile = lax.axis_index("tile") * tile_dev
    half_numbers = first_half + jnp.arange(half_dev, dtype=jnp.int32)
    angles = two_pi * (half_numbers.astype(jnp.float32)[:, None] + pulse_offset) / half_total
    waves = 0.5 + range_gates.astype(jnp.float32) / GATES
    shown = visible.astype(jnp.float32)
    half_count = echoes.shape[0]
    norm_scale = (2.0 * PULSE_H * FREQS) ** (-0.5)
    echo_piece = lax.all_gather(echoes, "tile", axis=1, tiled=True)
    wave_piece = lax.all_gather(waves, "tile", axis=1, tiled=True)
    angle_piece = lax.all_gather(angles, "tile", axis=1, tiled=True)
    stacked = []
    for half_slot in range(half_count):
        cosine_wave = (wave_piece[half_slot] * jnp.cos(angle_piece[half_slot])[:, None]).reshape(-1)
        sine_wave = (wave_piece[half_slot] * jnp.sin(angle_piece[half_slot])[:, None]).reshape(-1)
        echo_real = echo_piece[half_slot][:, :FREQS].reshape(-1)
        echo_imag = echo_piece[half_slot][:, FREQS:].reshape(-1)
        right_side = make_right(sine_wave)
        base_cos, base_sin = make_base(cosine_wave)
        tile_terms = []
        for tile_slot in range(tile_dev):

            def compute(
                echo_real=echo_real,
                echo_imag=echo_imag,
                cosine_wave=cosine_wave,
                sine_wave=sine_wave,
                base_cos=base_cos,
                base_sin=base_sin,
                right_side=right_side,
                tile_slot=tile_slot,
            ):
                left_side = make_left(
                    echo_real,
                    echo_imag,
                    cosine_wave,
                    sine_wave,
                    base_cos,
                    base_sin,
                    first_tile + tile_slot,
                    norm_scale,
                )
                return jnp.dot(left_side, right_side, preferred_element_type=jnp.float32)

            tile_term = compute()
            tile_terms.append(tile_term)
        stacked.append(jnp.stack(tile_terms))
    half_images = jnp.stack(stacked)
    half_images = half_images * shown[:, :, None, None]
    following = shifted(half_images[0], "sub", -1)
    successors = jnp.concatenate([half_images[1:half_dev], following[None]], axis=0)
    images = half_images + successors
    power_map = images[..., :PIX] ** 2 + images[..., PIX:] ** 2
    local_peak = jnp.max(power_map, axis=0)
    full_peak = lax.pmax(local_peak, "sub")
    row_count = PIX // sub_count
    peak = lax.dynamic_slice_in_dim(full_peak, lax.axis_index("sub") * row_count, row_count, 1)
    return (images, peak)


def solution(mesh):
    in_specs = (P("sub", "tile", None), P("sub", "tile"), P("sub", "tile", None), P("sub", "tile"))
    out_specs = (P("sub", "tile", None, None), P("tile", "sub", None))
    return jax.shard_map(
        on_device, mesh=mesh, in_specs=in_specs, out_specs=out_specs, check_vma=False
    )
```

profile of v0, /device:TPU:1, one launch (start us, length us, event | category | flops | bytes accessed | tf_op | source)
XLA Modules:
  0.0 301.1 jit_solution(487523907034118992)
XLA Ops:
  7.3 0.7 multiply_bitcast_fusion
  8.0 29.8 %all-gather = f32[32,1,2]{2,1,0:T(1,128)S(1)} all-gather(f32[1,1,2]{2,1,0:T(1,128)S(1)} %multiply_bitcast_fusion), channel_id=1, replica_groups=mesh['sub'=16,'tile'=32] {'tile'}, dimensions={0}, use_global_device_ids=true | all-gather | bytes 264 | tf_op jit(solution)/shard_map/all_gather | solution.py:67
  37.8 0.1 copy.9
  37.9 0.1 mul.1893
  38.0 0.1 mul.1894
  38.1 0.1 mul.1901
  38.3 0.1 mul.2051
  38.4 0.1 mul.2055
  38.5 29.0 %all_gather.9 = f32[2,32,128]{2,0,1:T(2,128)S(1)} all-gather(f32[2,1,128]{2,0,1:T(2,128)} %bitcast.94), channel_id=1, replica_groups=mesh['sub'=16,'tile'=32] {'tile'}, dimensions={1}, use_global_device_ids=true | all-gather | bytes 33792 | tf_op jit(solution)/shard_map/all_gather | solution.py:65
  67.5 0.1 fusion.122
  67.7 0.1 fusion.123
  67.9 0.7 multiply_add_fusion.16
  68.6 28.6 %all_gather.10 = f32[2,32,64]{2,0,1:T(2,128)S(1)} all-gather(f32[2,1,64]{2,0,1:T(2,128)S(1)} %multiply_add_fusion.16), channel_id=1, replica_groups=mesh['sub'=16,'tile'=32] {'tile'}, dimensions={1}, use_global_device_ids=true | all-gather | bytes 16896 | tf_op jit(solution)/shard_map/all_gather | solution.py:66
  97.2 0.1 slice_reduce_fusion.1
  97.3 0.1 squeeze.11
  97.4 0.1 subtract_multiply_fusion
  97.5 4.5 %sine_convert_fusion.1 = (bf16[2048,128]{1,0:T(8,128)(2,1)S(1)}, bf16[2048,128]{1,0:T(8,128)(2,1)S(1)}) fusion(f32[2048]{0:T(1024)S(1)} %get-tuple-element.117), kind=kLoop, calls=%fused_computation.125 | loop fusion | flops 786432 | bytes 1056768 | tf_op jit(solution)/shard_map/convert_element_type | solution.py:25
  102.0 4.1 %fusion.70 = bf16[2048,128]{1,0:T(8,128)(2,1)S(1)} fusion(f32[2048]{0:T(1024)S(1)} %get-tuple-element.117), kind=kLoop, calls=%fused_computation.133 | loop fusion | flops 1310720 | bytes 532480 | tf_op jit(solution)/shard_map/neg | solution.py:27
  106.3 0.3 add_multiply_fusion.8
  106.6 0.3 add_multiply_fusion
  106.8 4.5 %sine_convert_fusion = (bf16[2048,128]{1,0:T(8,128)(2,1)S(1)}, bf16[2048,128]{1,0:T(8,128)(2,1)S(1)}) fusion(f32[2048]{0:T(1024)S(1)} %get-tuple-element.9), kind=kLoop, calls=%fused_computation.103 | loop fusion | flops 786432 | bytes 1056768 | tf_op jit(solution)/shard_map/convert_element_type | solution.py:25
  111.3 4.1 %fusion.71 = bf16[2048,128]{1,0:T(8,128)(2,1)S(1)} fusion(f32[2048]{0:T(1024)S(1)} %get-tuple-element.9), kind=kLoop, calls=%fused_computation.134 | loop fusion | flops 1310720 | bytes 532480 | tf_op jit(solution)/shard_map/neg | solution.py:27
  115.4 6.3 %subtract_convert_fusion.8 = (bf16[128,2048]{1,0:T(8,128)(2,1)S(1)}, bf16[128,2048]{1,0:T(8,128)(2,1)S(1)}, bf16[128,2048]{1,0:T(8,128)(2,1)S(1)}, bf16[128,2048...) fusion(f32[2048]{0:T(1024)S(1)} %get-tuple-element.12, ...), kind=kLoop, calls=%fused_computation.112 | loop fusion | flops 17039360 | bytes 8527872 | tf_op jit(solution)/shard_map/convert.16
  121.7 0.5 fusion.15
  122.2 0.5 fusion.14
  122.6 0.5 fusion.13
  123.1 0.5 fusion.12
  123.6 0.5 fusion.11
  124.1 0.5 fusion.10
  124.6 0.5 fusion.9
  125.1 0.5 fusion.8
  125.6 6.2 %subtract_convert_fusion = (bf16[128,2048]{1,0:T(8,128)(2,1)S(1)}, bf16[128,2048]{1,0:T(8,128)(2,1)S(1)}, bf16[128,2048]{1,0:T(8,128)(2,1)S(1)}, bf16[128,2048]{...) fusion(f32[2048]{0:T(1024)S(1)} %get-tuple-element.29, ...), kind=kLoop, calls=%fused_computation.90 | loop fusion | flops 17039360 | bytes 8527872 | tf_op jit(solution)/shard_map/convert
  131.8 0.4 fusion.7
  132.2 0.4 fusion.6
  132.7 0.4 fusion.5
  133.1 0.4 fusion.4
  133.6 0.4 fusion.3
  134.0 0.5 fusion.2
  134.5 0.5 fusion.1
  135.0 0.5 fusion
  135.5 0.3 maximum_multiply_fusion
  135.7 0.2 fusion.120
  135.9 25.8 %collective-permute-start = (f32[8,128,256]{2,1,0:T(8,128)S(1)}, f32[8,128,256]{2,1,0:T(8,128)S(1)}, u32[]{:S(2)}, u32[]{:S(2)}) collective-permute-start(f32[8,128,256]{2,1,0:T(8,128)S(1)} %get-tuple-element.11), channel_id=1, source_target_pairs={{32,0},{64,32},{96,64},{128,96},{160,128},{192,160},{224,192},{256... | collective-permute-start | bytes 3145736 | tf_op jit(solution)/shard_map/ppermute | solution.py:18
  161.7 13.5 %collective-permute-done = f32[8,128,256]{2,1,0:T(8,128)S(1)} collective-permute-done((f32[8,128,256]{2,1,0:T(8,128)S(1)}, f32[8,128,256]{2,1,0:T(8,128)S(1)}, u32[]{:S(2)}, u32[]{:S(2)}) %collective-permute-start) | collective-permute-done | bytes 1048608 | tf_op jit(solution)/shard_map/ppermute | solution.py:18
  175.2 0.3 maximum_add_fusion
  175.6 1.1 fusion.17
  176.7 116.2 %all-reduce.2.cloned.1.call-done = f32[8,128,128]{2,1,0:T(8,128)} async-done(((f32[8,128,128]{2,1,0:T(8,128)}), f32[8,128,128]{2,1,0:T(8,128)}) %all-reduce.2.cloned.1.call-update) | async-done | bytes 524304 | tf_op jit(solution)/shard_map/pmax | solution.py:111
  292.9 1.4 constant_dynamic-slice_fusion
  (19 shorter events, 0.8 us)
Async XLA Ops:
  7.2 285.7 %all-reduce.2.cloned.1.call-start = ((), (), s32[]{:S(2)}) async-start(), calls=%async_computation | async-start | bytes 1048576 | tf_op jit(solution)/shard_map/pmax | solution.py:111
  67.7 47.7 %copy-start.1 = (s32[2,8]{1,0:T(2,128)S(1)}, s32[2,8]{1,0:T(2,128)}, u32[]{:S(2)}) copy-start(s32[2,8]{1,0:T(2,128)} %param.7) | copy-start | bytes 196
  135.9 39.3 %collective-permute-start = (f32[8,128,256]{2,1,0:T(8,128)S(1)}, f32[8,128,256]{2,1,0:T(8,128)S(1)}, u32[]{:S(2)}, u32[]{:S(2)}) collective-permute-start(f32[8,128,256]{2,1,0:T(8,128)S(1)} %get-tuple-element.11), channel_id=1, source_target_pairs={{32,0},{64,32},{96,64},{128,96},{160,128},{192,160},{224,192},{256... | collective-permute-start | bytes 3145736 | tf_op jit(solution)/shard_map/ppermute | solution.py:18
  175.6 118.7 %copy-start = (f32[2,8,128,256]{3,2,1,0:T(8,128)}, f32[2,8,128,256]{3,2,1,0:T(8,128)S(1)}, u32[]{:S(2)}) copy-start(f32[2,8,128,256]{3,2,1,0:T(8,128)S(1)} %maximum_add_fusion) | copy-start | bytes 6291460
Sparse Core Ops, SparseCore 0:
  176.8 116.0 all-reduce.1
where the time goes:
time: 301 us
  waiting for transfers between devices  130 us (43%)
  blocking collectives  87.4 us (29%)
  other arithmetic  33.3 us (11%)
  starting transfers between devices  25.8 us (9%)
  between operations  14.5 us (5%)
  matrix products  7.47 us (2%)
    pmax x1, waiting for transfers between devices, on_device(): full_peak = lax.pmax(local_peak, 'sub')  116 us
    all_gather x1, blocking collectives, on_device(): angle_piece = lax.all_gather(angles, 'tile', axis=1, tiled=True)  29.8 us
    all_gather x1, blocking collectives, on_device(): echo_piece = lax.all_gather(echoes, 'tile', axis=1, tiled=True)  29 us
    all_gather x1, blocking collectives, on_device(): wave_piece = lax.all_gather(waves, 'tile', axis=1, tiled=True)  28.6 us
    ppermute x1, starting transfers between devices, shifted(): return lax.ppermute(block, axis, route)  25.8 us
    ppermute x1, waiting for transfers between devices, shifted(): return lax.ppermute(block, axis, route)  13.5 us
    another operation x2, other arithmetic  12.5 us
    convert_element_type x2, other arithmetic, make_right(): imag_part = jnp.sin(phase_grid).astype(jnp.bfloat16)  8.92 us
  transfers between devices with their start and end apart: 2, of which 2 were waited for; matrix products, arithmetic and copies ran while one was open for 0% of the time, Pallas kernels for 0%

commit v1 on v0

--- a/solution.py
+++ b/solution.py
@@ -10,6 +10,14 @@
 GATES = 512
 grid_cols = 16
 two_pi = 2.0 * math.pi
+
+
+def tiled_gather(array, axis, dim):
+    size = lax.axis_size(axis)
+    repeats = [size if d == dim else 1 for d in range(array.ndim)]
+    return lax.all_to_all(
+        jnp.tile(array, repeats), axis, split_axis=dim, concat_axis=dim, tiled=True
+    )
 
 
 def shifted(block, axis, distance):
@@ -62,7 +70,7 @@
     shown = visible.astype(jnp.float32)
     half_count = echoes.shape[0]
     norm_scale = (2.0 * PULSE_H * FREQS) ** (-0.5)
-    echo_piece = lax.all_gather(echoes, "tile", axis=1, tiled=True)
+    echo_piece = tiled_gather(echoes, "tile", 1)
     wave_piece = lax.all_gather(waves, "tile", axis=1, tiled=True)
     angle_piece = lax.all_gather(angles, "tile", axis=1, tiled=True)
     stacked = []

time: 301 us -> 277 us (0.920)
  blocking collectives: 87.4 us -> 57.9 us
    all_gather x1 -> x0, blocking collectives: 29 us -> none  [on_device(): echo_piece = lax.all_gather(echoes, 'tile', axis=1, tiled=True)]
    all_to_all x0 -> x1, starting transfers between devices: none -> 10.5 us  [tiled_gather(): lax.all_to_all(jnp.tile(array, repeats), axis, split_axis=dim, concat_axi...]
    ppermute x1, starting transfers between devices: 25.8 us -> 16.7 us  [shifted(): return lax.ppermute(block, axis, route)]
  transfers between devices with their start and end apart: 2 -> 3, of which waited for: 2 -> 2; matrix products, arithmetic and copies ran while one was open for 0% -> 1% of each run, Pallas kernels for 0% -> 0%
where the time goes in v1:
time: 277 us; the launch traced here: 276 us
  waiting for transfers between devices  131 us (47%)
  blocking collectives  57.9 us (21%)
  other arithmetic  34.1 us (12%)
  starting transfers between devices  27.3 us (10%)
  between operations  14.4 us (5%)
  matrix products  7.58 us (3%)
  local copies, waits for them, and re-layouts  4.2 us (2%)
    pmax x1, waiting for transfers between devices, on_device(): full_peak = lax.pmax(local_peak, 'sub')  116 us
    all_gather x1, blocking collectives, on_device(): wave_piece = lax.all_gather(waves, 'tile', axis=1, tiled=True)  29.1 us
    all_gather x1, blocking collectives, on_device(): angle_piece = lax.all_gather(angles, 'tile', axis=1, tiled=True)  28.8 us
    ppermute x1, starting transfers between devices, shifted(): return lax.ppermute(block, axis, route)  16.7 us
    ppermute x1, waiting for transfers between devices, shifted(): return lax.ppermute(block, axis, route)  14.5 us
    another operation x2, other arithmetic  12.6 us
    all_to_all x1, starting transfers between devices, tiled_gather(): lax.all_to_all(jnp.tile(array, repeats), axis, split_axis=dim, concat_axi...  10.5 us
    convert_element_type x2, other arithmetic, make_right(): imag_part = jnp.sin(phase_grid).astype(jnp.bfloat16)  8.92 us
  transfers between devices with their start and end apart: 3, of which 2 were waited for; matrix products, arithmetic and copies ran while one was open for 1% of the time, Pallas kernels for 0%

profile of v1, /device:TPU:1, one launch (start us, length us, event | category | flops | bytes accessed | tf_op | source)
XLA Modules:
  0.0 276.3 jit_solution(10889975544962052204)
XLA Ops:
  7.2 1.3 tile.10
  8.5 10.5 %all-to-all-start = ((f32[2,32,128]{2,0,1:T(2,128)}), f32[2,32,128]{2,0,1:T(2,128)S(1)}, u32[]{:S(2)}, u32[]{:S(2)}) async-start(f32[2,32,128]{2,0,1:T(2,128)} %tile.10), calls=%async_computation | async-start | bytes 65536 | tf_op jit(solution)/shard_map/all_to_all | solution.py:18
  19.0 0.7 multiply_bitcast_fusion
  19.7 28.8 %all-gather = f32[32,1,2]{2,1,0:T(1,128)S(1)} all-gather(f32[1,1,2]{2,1,0:T(1,128)S(1)} %multiply_bitcast_fusion), channel_id=1, replica_groups=mesh['sub'=16,'tile'=32] {'tile'}, dimensions={0}, use_global_device_ids=true | all-gather | bytes 264 | tf_op jit(solution)/shard_map/all_gather | solution.py:75
  48.5 0.1 copy.8
  48.6 0.7 multiply_add_fusion.16
  49.3 29.1 %all_gather.6 = f32[2,32,64]{2,0,1:T(2,128)S(1)} all-gather(f32[2,1,64]{2,0,1:T(2,128)S(1)} %multiply_add_fusion.16), channel_id=1, replica_groups=mesh['sub'=16,'tile'=32] {'tile'}, dimensions={1}, use_global_device_ids=true | all-gather | bytes 16896 | tf_op jit(solution)/shard_map/all_gather | solution.py:74
  78.4 0.1 slice_reduce_fusion.1
  78.7 0.1 mul.1894
  78.8 0.1 mul.1901
  79.0 0.1 mul.2051
  79.1 0.1 mul.2055
  79.3 0.7 convert_element_type.130
  80.1 0.1 fusion.122
  80.3 0.1 fusion.123
  80.5 0.1 subtract_multiply_fusion
  80.6 4.5 %sine_convert_fusion.1 = (bf16[2048,128]{1,0:T(8,128)(2,1)S(1)}, bf16[2048,128]{1,0:T(8,128)(2,1)S(1)}) fusion(f32[2048]{0:T(1024)S(1)} %get-tuple-element.117), kind=kLoop, calls=%fused_computation.125 | loop fusion | flops 786432 | bytes 1056768 | tf_op jit(solution)/shard_map/convert_element_type | solution.py:33
  85.0 4.1 %fusion.70 = bf16[2048,128]{1,0:T(8,128)(2,1)S(1)} fusion(f32[2048]{0:T(1024)S(1)} %get-tuple-element.117), kind=kLoop, calls=%fused_computation.133 | loop fusion | flops 1310720 | bytes 532480 | tf_op jit(solution)/shard_map/neg | solution.py:35
  89.2 0.3 add_multiply_fusion.8
  89.5 0.3 add_multiply_fusion
  89.8 4.5 %sine_convert_fusion = (bf16[2048,128]{1,0:T(8,128)(2,1)S(1)}, bf16[2048,128]{1,0:T(8,128)(2,1)S(1)}) fusion(f32[2048]{0:T(1024)S(1)} %get-tuple-element.9), kind=kLoop, calls=%fused_computation.103 | loop fusion | flops 786432 | bytes 1056768 | tf_op jit(solution)/shard_map/convert_element_type | solution.py:33
  94.2 4.1 %fusion.71 = bf16[2048,128]{1,0:T(8,128)(2,1)S(1)} fusion(f32[2048]{0:T(1024)S(1)} %get-tuple-element.9), kind=kLoop, calls=%fused_computation.134 | loop fusion | flops 1310720 | bytes 532480 | tf_op jit(solution)/shard_map/neg | solution.py:35
  98.3 6.3 %subtract_convert_fusion.8 = (bf16[128,2048]{1,0:T(8,128)(2,1)S(1)}, bf16[128,2048]{1,0:T(8,128)(2,1)S(1)}, bf16[128,2048]{1,0:T(8,128)(2,1)S(1)}, bf16[128,2048...) fusion(f32[2048]{0:T(1024)S(1)} %get-tuple-element.12, ...), kind=kLoop, calls=%fused_computation.112 | loop fusion | flops 17039360 | bytes 8527872 | tf_op jit(solution)/shard_map/convert.16
  104.6 0.5 fusion.15
  105.1 0.5 fusion.14
  105.6 0.5 fusion.13
  106.1 0.5 fusion.12
  106.5 0.5 fusion.11
  107.0 0.5 fusion.10
  107.5 0.5 fusion.9
  108.0 0.5 fusion.8
  108.5 6.3 %subtract_convert_fusion = (bf16[128,2048]{1,0:T(8,128)(2,1)S(1)}, bf16[128,2048]{1,0:T(8,128)(2,1)S(1)}, bf16[128,2048]{1,0:T(8,128)(2,1)S(1)}, bf16[128,2048]{...) fusion(f32[2048]{0:T(1024)S(1)} %get-tuple-element.29, ...), kind=kLoop, calls=%fused_computation.90 | loop fusion | flops 17039360 | bytes 8527872 | tf_op jit(solution)/shard_map/convert
  114.7 0.5 fusion.7
  115.2 0.5 fusion.6
  115.7 0.5 fusion.5
  116.2 0.5 fusion.4
  116.7 0.5 fusion.3
  117.2 0.5 fusion.2
  117.7 0.5 fusion.1
  118.2 0.4 fusion
  118.6 0.3 maximum_multiply_fusion
  118.9 0.1 fusion.120
  119.0 16.7 %collective-permute-start = (f32[8,128,256]{2,1,0:T(8,128)S(1)}, f32[8,128,256]{2,1,0:T(8,128)S(1)}, u32[]{:S(2)}, u32[]{:S(2)}) collective-permute-start(f32[8,128,256]{2,1,0:T(8,128)S(1)} %get-tuple-element.11), channel_id=1, source_target_pairs={{32,0},{64,32},{96,64},{128,96},{160,128},{192,160},{224,192},{256... | collective-permute-start | bytes 3145736 | tf_op jit(solution)/shard_map/ppermute | solution.py:26
  135.7 14.5 %collective-permute-done = f32[8,128,256]{2,1,0:T(8,128)S(1)} collective-permute-done((f32[8,128,256]{2,1,0:T(8,128)S(1)}, f32[8,128,256]{2,1,0:T(8,128)S(1)}, u32[]{:S(2)}, u32[]{:S(2)}) %collective-permute-start) | collective-permute-done | bytes 1048608 | tf_op jit(solution)/shard_map/ppermute | solution.py:26
  150.2 0.3 maximum_add_fusion
  150.6 1.1 fusion.17
  151.7 116.4 %all-reduce.2.cloned.1.call-done = f32[8,128,128]{2,1,0:T(8,128)} async-done(((f32[8,128,128]{2,1,0:T(8,128)}), f32[8,128,128]{2,1,0:T(8,128)}) %all-reduce.2.cloned.1.call-update) | async-done | bytes 524304 | tf_op jit(solution)/shard_map/pmax | solution.py:119
  268.0 1.4 constant_dynamic-slice_fusion
  (19 shorter events, 1.0 us)
Async XLA Ops:
  8.5 71.6 %all-to-all-start = ((f32[2,32,128]{2,0,1:T(2,128)}), f32[2,32,128]{2,0,1:T(2,128)S(1)}, u32[]{:S(2)}, u32[]{:S(2)}) async-start(f32[2,32,128]{2,0,1:T(2,128)} %tile.10), calls=%async_computation | async-start | bytes 65536 | tf_op jit(solution)/shard_map/all_to_all | solution.py:18
  19.0 249.1 %all-reduce.2.cloned.1.call-start = ((), (), s32[]{:S(2)}) async-start(), calls=%async_computation.1 | async-start | bytes 1048576 | tf_op jit(solution)/shard_map/pmax | solution.py:119
  119.0 31.2 %collective-permute-start = (f32[8,128,256]{2,1,0:T(8,128)S(1)}, f32[8,128,256]{2,1,0:T(8,128)S(1)}, u32[]{:S(2)}, u32[]{:S(2)}) collective-permute-start(f32[8,128,256]{2,1,0:T(8,128)S(1)} %get-tuple-element.11), channel_id=1, source_target_pairs={{32,0},{64,32},{96,64},{128,96},{160,128},{192,160},{224,192},{256... | collective-permute-start | bytes 3145736 | tf_op jit(solution)/shard_map/ppermute | solution.py:26
  150.6 118.9 %copy-start = (f32[2,8,128,256]{3,2,1,0:T(8,128)}, f32[2,8,128,256]{3,2,1,0:T(8,128)S(1)}, u32[]{:S(2)}) copy-start(f32[2,8,128,256]{3,2,1,0:T(8,128)S(1)} %maximum_add_fusion) | copy-start | bytes 6291460
Sparse Core Ops, SparseCore 0:
  151.8 116.1 all-reduce.1
